TPU v7x, 256 devices: a whole 4x4x8 slice. The times are simulated.
256 devices in a mesh: dp: 32 (over x, z), comp: 8 (over y, core).
Axes of the slice: x: 4, y: 4, z: 8, core: 2. Of those that a mesh axis runs over, the one named last changes fastest.
Arguments:
- embeddings: float32 [32768, 1024], P('dp'), may hold values from -6 to 6
- means: float32 [8192, 1024], P(('comp', 'dp')), may hold values from -2 to 2
- variances: float32 [8192, 1024], P(('comp', 'dp')), may hold values from 0.7 to 1.4
- log_weights: float32 [8192], P(('comp', 'dp')), may hold values from -2 to 0
Outputs:
- new_means: float32 [8192, 1024], P(('comp', 'dp'))
- new_variances: float32 [8192, 1024], P(('comp', 'dp'))
- new_weights: float32 [8192], P(('comp', 'dp'))
- row_loglik: float32 [32768], P('dp')
All inputs are finite; a program needn't handle non-finite values.
Results may differ from a plain program's by a relative error of at most 0.00045.
Values sent between devices are 32-bit elements; how exact they have to be, the bound alone decides.
A program may use at most 128 MiB of HBM per device.

v0:
```python
import jax
import jax.numpy as jnp
from jax import lax
from jax.sharding import PartitionSpec as P

circle_log = 1.8378770664093453


def component_terms(means, variances, log_weights):
    precision = 1.0 / variances
    scaled = means * precision
    width = means.shape[1]
    offset = (
        log_weights
        - 0.5 * jnp.sum(jnp.log(variances), axis=1)
        - 0.5 * jnp.sum(means * scaled, axis=1)
        - 0.5 * width * circle_log
    )
    return (precision, scaled, offset)


def row_scores(block, squares, precision, scaled, offset):
    highest = lax.Precision.HIGHEST
    quad = jnp.dot(squares, precision.T, precision=highest, preferred_element_type=jnp.float32)
    cross = jnp.dot(block, scaled.T, precision=highest, preferred_element_type=jnp.float32)
    return offset[None, :] + cross - 0.5 * quad


def weighted_sum(resp, values):
    return lax.dot_general(
        resp,
        values,
        (((0,), (0,)), ((), ())),
        precision=lax.Precision.HIGHEST,
        preferred_element_type=jnp.float32,
    )


def per_device(embeddings, means, variances, log_weights):
    squares = embeddings * embeddings
    precision, scaled, offset = component_terms(
        lax.all_gather(means, "dp", axis=0, tiled=True),
        lax.all_gather(variances, "dp", axis=0, tiled=True),
        lax.all_gather(log_weights, "dp", axis=0, tiled=True),
    )
    scores = row_scores(embeddings, squares, precision, scaled, offset)
    local_peak = jnp.max(scores, axis=1)
    peak = lax.pmax(local_peak, "comp")
    total = lax.psum(jnp.sum(jnp.exp(scores - peak[:, None]), axis=1), "comp")
    row_loglik = peak + jnp.log(total)
    resp = jnp.exp(scores - row_loglik[:, None])
    summed = lax.psum_scatter(
        jnp.concatenate([weighted_sum(resp, embeddings), weighted_sum(resp, squares)], axis=1),
        "dp",
        scatter_dimension=0,
        tiled=True,
    )
    counts = lax.psum_scatter(jnp.sum(resp, axis=0), "dp", scatter_dimension=0, tiled=True)
    width = embeddings.shape[1]
    first = summed[:, :width]
    second = summed[:, width:]
    denom = (counts + 1.0)[:, None]
    new_means = (first + means) / denom
    new_variances = (second + variances + means * means) / denom - new_means * new_means
    new_weights = counts / (embeddings.shape[0] * lax.axis_size("dp"))
    return (new_means, new_variances, new_weights, row_loglik)


def solution(mesh):
    return jax.shard_map(
        per_device,
        mesh=mesh,
        in_specs=(
            P("dp", None),
            P(("comp", "dp"), None),
            P(("comp", "dp"), None),
            P(("comp", "dp")),
        ),
        out_specs=(P(("comp", "dp"), None), P(("comp", "dp"), None), P(("comp", "dp")), P("dp")),
        check_vma=False,
    )
```

profile of v0, /device:TPU:8, one launch (start us, length us, event | category | flops | bytes accessed | tf_op | source)
XLA Modules:
  0.0 516.7 jit_solution(10036778705342761832)
XLA Ops:
  7.2 0.0 all-gather.5.cloned.1.call-start
  7.2 0.7 all-gather.5.cloned.1.call-update
  7.9 0.0 all-gather.3.cloned.1.call-start
  7.9 0.7 all-gather.3.cloned.1.call-update
  8.6 0.0 reduce-scatter.4.cloned.1.call-start
  8.7 1.3 fusion.17
  10.7 0.9 dynamic-update-slice
  11.6 78.0 %all-reduce = f32[1024]{0:T(1024)S(1)} all-reduce(f32[1024]{0:T(1024)S(1)} %dynamic-update-slice), channel_id=1, replica_groups=mesh['dp'=32,'comp'=8] {'dp'}, use_global_device_ids=true, to_apply=%add | all-reduce | flops 1024 | bytes 8192
  89.6 5.7 %all-gather.5.cloned.1.call-done = f32[1024,1024]{1,0:T(8,128)} async-done(((f32[32,1024]{1,0:T(8,128)}), f32[1024,1024]{1,0:T(8,128)}) %all-gather.5.cloned.1.call-update) | async-done | bytes 4194320 | tf_op jit(solution)/shard_map/all_gather | solution.py:42
  95.3 81.7 %all-gather.3.cloned.1.call-done = f32[1024,1024]{1,0:T(8,128)} async-done(((f32[32,1024]{1,0:T(8,128)}), f32[1024,1024]{1,0:T(8,128)}) %all-gather.3.cloned.1.call-update) | async-done | bytes 4194320 | tf_op jit(solution)/shard_map/all_gather | solution.py:43
  177.0 0.0 copy-start.2
  177.0 0.0 copy-start.6
  177.0 5.1 log_reduce_fusion
  182.1 0.0 copy-done.2
  182.1 0.7 copy-done.6
  182.9 0.0 copy-start.1
  182.9 13.6 %fusion.2 = f32[1024,1024]{0,1:T(8,128)S(1)} fusion(f32[1024,1024]{1,0:T(8,128)S(1)} %copy-done.6, f32[1024,1024]{1,0:T(8,128)S(1)} %copy-done.2), kind=kOutput, calls=%fused_computation.8 | convolution fusion | flops 12886999040 | bytes 12582912 | tf_op jit(solution)/shard_map/dot_general | solution.py:24
  196.4 0.0 copy-done.1
  196.4 15.2 %fusion.18 = (f32[1024]{0:T(1024)S(1)}, f32[1024,1024]{0,1:T(8,128)}) fusion(f32[1024,1024]{0,1:T(8,128)S(1)} %fusion.2, f32[1024,1024]{1,0:T(8,128)S(1)} %copy-done.6, f32[1024,1024]{1,0:T(8,128)S(1)} %copy-done.1, f32[1024,1024]{1,0:T(8,128)S(1)} %copy-done.2, f32[1024]{0:T(1024)S(1)} %subtract_add_fusion), kind=kOutput, calls=%fused_computation.28 | convolution fusion | flops 12891192320 | bytes 20979712 | tf_op jit(solution)/shard_map/dot_general | solution.py:25
  211.7 10.0 %pmax.7 = f32[1024]{0:T(1024)S(1)} all-reduce(f32[1024]{0:T(1024)S(1)} %get-tuple-element.20), channel_id=1, replica_groups=mesh['dp'=32,'comp'=8] {'comp'}, use_global_device_ids=true, to_apply=%region_3.0 | all-reduce | flops 1024 | bytes 8192 | tf_op jit(solution)/shard_map/pmax | solution.py:48
  221.6 2.8 exponential_reduce_fusion
  224.4 12.4 %psum.7 = f32[1024]{0:T(1024)S(1)} all-reduce(f32[1024]{0:T(1024)S(1)} %exponential_reduce_fusion), channel_id=1, replica_groups=mesh['dp'=32,'comp'=8] {'comp'}, use_global_device_ids=true, to_apply=%region_5.0 | all-reduce | flops 1024 | bytes 8192 | tf_op jit(solution)/shard_map/psum | solution.py:49
  236.9 0.0 copy-start.5
  236.9 0.0 copy-start
  236.9 0.0 copy-start.7
  236.9 17.7 %fusion = f32[1024,1024]{0,1:T(8,128)S(1)} fusion(f32[1024,1024]{1,0:T(8,128)} %param.4, f32[1024,1024]{0,1:T(8,128)} %get-tuple-element.21, f32[1024]{0:T(1024)S(1)} %log_add_fusion), kind=kOutput, calls=%fused_computation.6 | convolution fusion | flops 12886999040 | bytes 12587008 | tf_op jit(solution)/shard_map/dot_general | solution.py:30
  254.6 0.0 copy-done
  254.6 0.0 copy-done.7
  254.6 13.8 %fusion.7 = f32[1024,1024]{0,1:T(8,128)S(1)} fusion(f32[1024,1024]{1,0:T(8,128)S(1)} %copy-done.7, f32[1024,1024]{0,1:T(8,128)S(1)} %copy-done, f32[1024]{0:T(1024)S(1)} %log_add_fusion), kind=kOutput, calls=%fused_computation.13 | convolution fusion | flops 12885950464 | bytes 12587008 | tf_op jit(solution)/shard_map/dot_general | solution.py:30
  268.5 4.1 pad_maximum_fusion
  272.5 9.1 %copy.22 = f32[1024,2048]{1,0:T(8,128)} copy(f32[1024,2048]{0,1:T(8,128)} %pad_maximum_fusion) | data formatting | bytes 16777216
  281.7 0.0 reduce-scatter.4.cloned.1.call-update
  281.7 0.0 copy-start.3
  281.7 0.0 copy-start.4
  282.4 0.0 copy-done.5
  282.4 2.8 fusion.6
  285.2 72.8 %all-reduce.1 = f32[1024]{0:T(1024)S(1)} all-reduce(f32[1024]{0:T(1024)S(1)} %fusion.6), channel_id=3, replica_groups=mesh['dp'=32,'comp'=8] {'dp'}, use_global_device_ids=true, to_apply=%region_8.0.clone | all-reduce | flops 1024 | bytes 8192
  358.0 0.6 broadcast_multiply_fusion
  358.6 149.4 %reduce-scatter.4.cloned.1.call-done = f32[32,2048]{1,0:T(8,128)} async-done(((f32[1024,2048]{1,0:T(8,128)}), f32[32,2048]{1,0:T(8,128)}) %reduce-scatter.4.cloned.1.call-update) | async-done | bytes 262160 | tf_op jit(solution)/shard_map/reduce_scatter | solution.py:52
  507.9 0.0 copy-done.3
  507.9 0.0 copy-done.4
  507.9 1.8 fusion.14
  (3 shorter events, 0.0 us)
Async XLA Ops:
  7.2 88.1 %all-gather.5.cloned.1.call-start = ((), (), s32[]{:S(2)}) async-start(), calls=%async_computation.2 | async-start | bytes 4325376 | tf_op jit(solution)/shard_map/all_gather | solution.py:42
  7.9 169.1 %all-gather.3.cloned.1.call-start = ((), (), s32[]{:S(2)}) async-start(), calls=%async_computation.1 | async-start | bytes 4325376 | tf_op jit(solution)/shard_map/all_gather | solution.py:43
  8.6 499.3 %reduce-scatter.4.cloned.1.call-start = ((), (), s32[]{:S(2)}) async-start(), calls=%async_computation.3 | async-start | bytes 8650752 | tf_op jit(solution)/shard_map/reduce_scatter | solution.py:52
  177.0 5.2 copy-start.2
  177.0 5.9 %copy-start.6 = (f32[1024,1024]{1,0:T(8,128)S(1)}, f32[1024,1024]{1,0:T(8,128)}, u32[]{:S(2)}) copy-start(f32[1024,1024]{1,0:T(8,128)} %param.4) | copy-start | bytes 12582916
  182.9 13.6 %copy-start.1 = (f32[1024,1024]{1,0:T(8,128)S(1)}, f32[1024,1024]{1,0:T(8,128)}, u32[]{:S(2)}) copy-start(f32[1024,1024]{1,0:T(8,128)} %all-gather.5.cloned.1.call-done) | copy-start | bytes 12582916
  236.9 45.5 %copy-start.5 = (f32[1024]{0:T(1024)}, f32[1024]{0:T(1024)S(1)}, u32[]{:S(2)}) copy-start(f32[1024]{0:T(1024)S(1)} %log_add_fusion) | copy-start | bytes 12292
  236.9 17.7 %copy-start = (f32[1024,1024]{0,1:T(8,128)S(1)}, f32[1024,1024]{0,1:T(8,128)}, u32[]{:S(2)}) copy-start(f32[1024,1024]{0,1:T(8,128)} %get-tuple-element.21) | copy-start | bytes 12582916
  236.9 17.7 %copy-start.7 = (f32[1024,1024]{1,0:T(8,128)S(1)}, f32[1024,1024]{1,0:T(8,128)}, u32[]{:S(2)}) copy-start(f32[1024,1024]{1,0:T(8,128)} %param.4) | copy-start | bytes 12582916
  281.7 226.3 %copy-start.3 = (f32[32,1024]{1,0:T(8,128)S(1)}, f32[32,1024]{1,0:T(8,128)}, u32[]{:S(2)}) copy-start(f32[32,1024]{1,0:T(8,128)} %param.6) | copy-start | bytes 393220
  281.7 226.2 %copy-start.4 = (f32[32,1024]{1,0:T(8,128)S(1)}, f32[32,1024]{1,0:T(8,128)}, u32[]{:S(2)}) copy-start(f32[32,1024]{1,0:T(8,128)} %param.5) | copy-start | bytes 393220
Sparse Core Ops, SparseCore 0:
  10.6 84.6 all-gather.4
  97.9 79.0 all-gather.2
  281.8 226.0 reduce-scatter.3
where the time goes:
time: 526 us; the launch traced here: 517 us
  waiting for transfers between devices  238 us (45%)
  blocking collectives  173 us (33%)
  matrix products  60.3 us (11%)
  other arithmetic  17.2 us (3%)
  between operations  15.7 us (3%)
  local copies, waits for them, and re-layouts  12.1 us (2%)
    unnamed x2, blocking collectives  151 us
    reduce_scatter x1, waiting for transfers between devices, per_device(): lax.psum_scatter(jnp.concatenate([weighted_sum(resp, embeddings), weighte...  149 us
    all_gather x1, waiting for transfers between devices, per_device(): lax.all_gather(variances, 'dp', axis=0, tiled=True)  81.7 us
    dot_general x2, matrix products, weighted_sum(): lax.dot_general(resp, values, (((0,), (0,)), ((), ())), precision=lax.Pre...  31.5 us
    dot_general x1, matrix products, row_scores(): jnp.dot(block, scaled.T, precision=highest, preferred_element_type=jnp.fl...  15.2 us
    dot_general x1, matrix products, row_scores(): jnp.dot(squares, precision.T, precision=highest, preferred_element_type=j...  13.6 us
    psum x1, blocking collectives, per_device(): total = lax.psum(jnp.sum(jnp.exp(scores - peak[:, None]), axis=1), 'comp')  12.4 us
    unnamed x20, local copies, waits for them, and re-layouts  12.1 us
  transfers between devices with their start and end apart: 3, of which 3 were waited for; matrix products, arithmetic and copies ran while one was open for 1% of the time, Pallas kernels for 0%

commit v1 on v0

--- a/solution.py
+++ b/solution.py
@@ -40,7 +40,9 @@
     squares = embeddings * embeddings
     precision, scaled, offset = component_terms(
         lax.all_gather(means, "dp", axis=0, tiled=True),
-        lax.all_gather(variances, "dp", axis=0, tiled=True),
+        jnp.concatenate(
+            lax.all_to_all(jnp.stack([variances] * lax.axis_size("dp")), "dp", 0, 0), axis=0
+        ),
         lax.all_gather(log_weights, "dp", axis=0, tiled=True),
     )
     scores = row_scores(embeddings, squares, precision, scaled, offset)

time: 526 us -> 550 us (1.046)
  blocking collectives: 173 us -> 263 us
  waiting for transfers between devices: 238 us -> 148 us
  starting transfers between devices: 0.11 us -> 11.7 us
  matrix products: 60.3 us -> 67.1 us
    unnamed x2, blocking collectives: 151 us -> 240 us
    all_gather x1 -> x0, waiting for transfers between devices: 81.7 us -> none  [per_device(): lax.all_gather(variances, 'dp', axis=0, tiled=True)]
    all_to_all x0 -> x1, starting transfers between devices: none -> 11.6 us  [per_device(): lax.all_to_all(jnp.stack([variances] * lax.axis_size('dp')), 'dp', 0, 0)]
    all_gather x1, waiting for transfers between devices: 5.66 us -> 0.01 us  [per_device(): lax.all_gather(means, 'dp', axis=0, tiled=True)]
    unnamed x20 -> x22, local copies, waits for them, and re-layouts: 12.1 us -> 11.8 us
  transfers between devices with their start and end apart: 3 -> 3, of which waited for: 3 -> 1; matrix products, arithmetic and copies ran while one was open for 1% -> 5% of each run, Pallas kernels for 0% -> 0%
where the time goes in v1:
time: 550 us; the launch traced here: 542 us
  blocking collectives  263 us (48%)
  waiting for transfers between devices  148 us (27%)
  matrix products  67.1 us (12%)
  other arithmetic  21.4 us (4%)
  between operations  15.8 us (3%)
  local copies, waits for them, and re-layouts  15.3 us (3%)
  starting transfers between devices  11.7 us (2%)
    unnamed x2, blocking collectives  240 us
    reduce_scatter x1, waiting for transfers between devices, per_device(): lax.psum_scatter(jnp.concatenate([weighted_sum(resp, embeddings), weighte...  148 us
    dot_general x2, matrix products, weighted_sum(): lax.dot_general(resp, values, (((0,), (0,)), ((), ())), precision=lax.Pre...  31.6 us
    dot_general x1, matrix products, row_scores(): jnp.dot(block, scaled.T, precision=highest, preferred_element_type=jnp.fl...  17.8 us
    dot_general x1, matrix products, row_scores(): jnp.dot(squares, precision.T, precision=highest, preferred_element_type=j...  17.7 us
    psum x1, blocking collectives, per_device(): total = lax.psum(jnp.sum(jnp.exp(scores - peak[:, None]), axis=1), 'comp')  12.4 us
    unnamed x22, local copies, waits for them, and re-layouts  11.8 us
    all_to_all x1, starting transfers between devices, per_device(): lax.all_to_all(jnp.stack([variances] * lax.axis_size('dp')), 'dp', 0, 0)  11.6 us
  transfers between devices with their start and end apart: 3, of which 1 were waited for; matrix products, arithmetic and copies ran while one was open for 5% of the time, Pallas kernels for 0%

profile of v1, /device:TPU:8, one launch (start us, length us, event | category | flops | bytes accessed | tf_op | source)
XLA Modules:
  0.0 542.3 jit_solution(5614488161369537016)
XLA Ops:
  7.2 3.4 stack.2
  10.6 0.0 copy-start.7
  10.6 0.0 copy-start.8
  10.6 11.6 %all-to-all-start = ((f32[32,32,1024]{2,1,0:T(8,128)}), f32[32,32,1024]{2,1,0:T(8,128)}, u32[]{:S(2)}, u32[]{:S(2)}) async-start(f32[32,32,1024]{2,1,0:T(8,128)} %stack.2), calls=%async_computation | async-start | bytes 8388608 | tf_op jit(solution)/shard_map/all_to_all | solution.py:44
  22.2 0.0 all-gather.2.cloned.1.call-start
  22.2 0.7 all-gather.2.cloned.1.call-update
  22.9 0.0 reduce-scatter.4.cloned.1.call-start
  22.9 0.0 copy-done.7
  23.0 0.6 fusion.17
  24.2 0.0 copy-done.8
  24.2 0.2 dynamic-update-slice
  24.5 170.2 %all-reduce = f32[1024]{0:T(1024)S(1)} all-reduce(f32[1024]{0:T(1024)S(1)} %dynamic-update-slice), channel_id=1, replica_groups=mesh['dp'=32,'comp'=8] {'dp'}, use_global_device_ids=true, to_apply=%add | all-reduce | flops 1024 | bytes 8192
  194.7 0.0 all-to-all-done
  194.7 5.2 log_reduce_fusion
  199.9 0.1 mul.31
  200.0 17.7 %fusion.2 = f32[1024,1024]{0,1:T(8,128)} fusion(f32[1024,1024]{1,0:T(8,128)} %bitcast.10, f32[1024,1024]{1,0:T(8,128)} %param.4), kind=kOutput, calls=%fused_computation.8 | convolution fusion | flops 12885950464 | bytes 12582912 | tf_op jit(solution)/shard_map/dot_general | solution.py:24
  217.7 0.0 all-gather.2.cloned.1.call-done
  217.7 0.0 copy-start.1
  217.7 0.0 copy-start.2
  217.7 4.1 multiply_reduce_fusion
  221.8 0.5 copy-done.1
  222.4 1.3 copy-done.2
  223.7 17.8 %fusion.18 = (f32[1024]{0:T(1024)S(1)}, f32[1024,1024]{0,1:T(8,128)}) fusion(f32[1024,1024]{0,1:T(8,128)} %fusion.2, f32[1024,1024]{1,0:T(8,128)} %param.4, f32[1024,1024]{1,0:T(8,128)S(1)} %copy-done.2, f32[1024,1024]{1,0:T(8,128)S(1)} %bitcast.11, f32[1024]{0:T(1024)S(1)} %subtract_add_fusion), kind=kOutput, calls=%fused_computation.29 | convolution fusion | flops 12890143744 | bytes 20979712 | tf_op jit(solution)/shard_map/dot_general | solution.py:25
  241.4 10.0 %pmax.7 = f32[1024]{0:T(1024)S(1)} all-reduce(f32[1024]{0:T(1024)S(1)} %get-tuple-element.20), channel_id=1, replica_groups=mesh['dp'=32,'comp'=8] {'comp'}, use_global_device_ids=true, to_apply=%region_3.0 | all-reduce | flops 1024 | bytes 8192 | tf_op jit(solution)/shard_map/pmax | solution.py:50
  251.4 2.8 exponential_reduce_fusion
  254.2 12.4 %psum.7 = f32[1024]{0:T(1024)S(1)} all-reduce(f32[1024]{0:T(1024)S(1)} %exponential_reduce_fusion), channel_id=1, replica_groups=mesh['dp'=32,'comp'=8] {'comp'}, use_global_device_ids=true, to_apply=%region_5.0 | all-reduce | flops 1024 | bytes 8192 | tf_op jit(solution)/shard_map/psum | solution.py:51
  266.6 0.0 copy-start.6
  266.6 0.0 copy-start
  266.6 0.0 copy-start.3
  266.6 17.8 %fusion = f32[1024,1024]{0,1:T(8,128)S(1)} fusion(f32[1024,1024]{1,0:T(8,128)} %param.4, f32[1024,1024]{0,1:T(8,128)} %get-tuple-element.21, f32[1024]{0:T(1024)S(1)} %log_add_fusion), kind=kOutput, calls=%fused_computation.6 | convolution fusion | flops 12886999040 | bytes 12587008 | tf_op jit(solution)/shard_map/dot_general | solution.py:30
  284.5 0.0 copy-done
  284.5 0.0 copy-done.3
  284.5 13.8 %fusion.7 = f32[1024,1024]{0,1:T(8,128)S(1)} fusion(f32[1024,1024]{1,0:T(8,128)S(1)} %copy-done.3, f32[1024,1024]{0,1:T(8,128)S(1)} %copy-done, f32[1024]{0:T(1024)S(1)} %log_add_fusion), kind=kOutput, calls=%fused_computation.13 | convolution fusion | flops 12885950464 | bytes 12587008 | tf_op jit(solution)/shard_map/dot_general | solution.py:30
  298.3 4.1 pad_maximum_fusion
  302.4 9.1 %copy.22 = f32[1024,2048]{1,0:T(8,128)} copy(f32[1024,2048]{0,1:T(8,128)} %pad_maximum_fusion) | data formatting | bytes 16777216
  311.5 0.0 reduce-scatter.4.cloned.1.call-update
  311.5 0.0 copy-start.4
  311.6 0.0 copy-start.5
  312.3 0.0 copy-done.6
  312.3 2.8 fusion.6
  315.1 70.1 %all-reduce.1 = f32[1024]{0:T(1024)S(1)} all-reduce(f32[1024]{0:T(1024)S(1)} %fusion.6), channel_id=3, replica_groups=mesh['dp'=32,'comp'=8] {'dp'}, use_global_device_ids=true, to_apply=%region_8.0.clone | all-reduce | flops 1024 | bytes 8192
  385.1 0.6 broadcast_multiply_fusion.1
  385.7 147.7 %reduce-scatter.4.cloned.1.call-done = f32[32,2048]{1,0:T(8,128)} async-done(((f32[1024,2048]{1,0:T(8,128)}), f32[32,2048]{1,0:T(8,128)}) %reduce-scatter.4.cloned.1.call-update) | async-done | bytes 262160 | tf_op jit(solution)/shard_map/reduce_scatter | solution.py:54
  533.4 0.0 copy-done.4
  533.4 0.0 copy-done.5
  533.4 1.8 fusion.14
  (4 shorter events, 0.0 us)
Async XLA Ops:
  10.6 12.4 %copy-start.7 = (u32[256]{0:T(256)S(1)}, u32[256]{0:T(256)}, u32[]{:S(2)}) copy-start(u32[256]{0:T(256)} %constant.21) | copy-start | bytes 3076
  10.6 13.6 %copy-start.8 = (f32[32]{0:T(128)S(1)}, f32[32]{0:T(128)}, u32[]{:S(2)}) copy-start(f32[32]{0:T(128)} %param.7) | copy-start | bytes 388
  10.6 184.1 %all-to-all-start = ((f32[32,32,1024]{2,1,0:T(8,128)}), f32[32,32,1024]{2,1,0:T(8,128)}, u32[]{:S(2)}, u32[]{:S(2)}) async-start(f32[32,32,1024]{2,1,0:T(8,128)} %stack.2), calls=%async_computation | async-start | bytes 8388608 | tf_op jit(solution)/shard_map/all_to_all | solution.py:44
  22.2 195.6 %all-gather.2.cloned.1.call-start = ((), (), s32[]{:S(2)}) async-start(), calls=%async_computation.2 | async-start | bytes 4325376 | tf_op jit(solution)/shard_map/all_gather | solution.py:42
  22.9 510.5 %reduce-scatter.4.cloned.1.call-start = ((), (), s32[]{:S(2)}) async-start(), calls=%async_computation.3 | async-start | bytes 8650752 | tf_op jit(solution)/shard_map/reduce_scatter | solution.py:54
  217.7 4.6 copy-start.1
  217.7 5.9 %copy-start.2 = (f32[1024,1024]{1,0:T(8,128)S(1)}, f32[1024,1024]{1,0:T(8,128)}, u32[]{:S(2)}) copy-start(f32[1024,1024]{1,0:T(8,128)} %all-gather.2.cloned.1.call-done) | copy-start | bytes 12582916
  266.6 45.6 %copy-start.6 = (f32[1024]{0:T(1024)}, f32[1024]{0:T(1024)S(1)}, u32[]{:S(2)}) copy-start(f32[1024]{0:T(1024)S(1)} %log_add_fusion) | copy-start | bytes 12292
  266.6 17.8 %copy-start = (f32[1024,1024]{0,1:T(8,128)S(1)}, f32[1024,1024]{0,1:T(8,128)}, u32[]{:S(2)}) copy-start(f32[1024,1024]{0,1:T(8,128)} %get-tuple-element.21) | copy-start | bytes 12582916
  266.6 17.8 %copy-start.3 = (f32[1024,1024]{1,0:T(8,128)S(1)}, f32[1024,1024]{1,0:T(8,128)}, u32[]{:S(2)}) copy-start(f32[1024,1024]{1,0:T(8,128)} %param.4) | copy-start | bytes 12582916
  311.5 221.9 %copy-start.4 = (f32[32,1024]{1,0:T(8,128)S(1)}, f32[32,1024]{1,0:T(8,128)}, u32[]{:S(2)}) copy-start(f32[32,1024]{1,0:T(8,128)} %param.6) | copy-start | bytes 393220
  311.6 221.8 %copy-start.5 = (f32[32,1024]{1,0:T(8,128)S(1)}, f32[32,1024]{1,0:T(8,128)}, u32[]{:S(2)}) copy-start(f32[32,1024]{1,0:T(8,128)} %param.5) | copy-start | bytes 393220
Sparse Core Ops, SparseCore 0:
  25.6 118.4 all-gather.1
  311.7 221.6 reduce-scatter.3
